TPU v7x, 256 devices: a whole 4x4x8 slice. The times are simulated.
256 devices in a mesh: seq: 16 (over z, core), pipe: 4 (over y), dp: 4 (over x).
Axes of the slice: x: 4, y: 4, z: 8, core: 2. Of those that a mesh axis runs over, the one named last changes fastest.
Arguments:
- segment_input: bfloat16 [4, 4096, 3072], P('pipe', ('dp', 'seq')), parts along dimension 1
- output_grad: bfloat16 [4, 4096, 3072], P('pipe', ('dp', 'seq')), parts along dimension 1, may hold values from -6 to 6
- qkv_weight: bfloat16 [4, 3072, 16, 384], P('pipe', None, 'seq')
- out_weight: bfloat16 [4, 2048, 3072], P('pipe', 'seq'), may hold values from -0.125 to 0.125
- query_gain: float32 [4, 128], P('pipe')
- key_gain: float32 [4, 128], P('pipe')
- gate_scale: float32 [4, 3072], P('pipe'), may hold values from -4 to 4
- neighbours: int32 [64, 27], P('dp'), parts along dimension 0, may hold values from -1 to 15
- tile_slot: int32 [64], P('dp'), parts along dimension 0, may hold values from 0 to 15, as said below
Outputs:
- segment_output: bfloat16 [4, 4096, 3072], P('pipe', ('dp', 'seq')), parts along dimension 1
- input_grad: bfloat16 [4, 4096, 3072], P('pipe', ('dp', 'seq')), parts along dimension 1
- gate_grad: float32 [16, 3072], P(('dp', 'pipe'), 'seq'), parts along dimension 0
There are 4 independent parts, one for each index of `dp`. A program takes and returns all parts, laid end to end along the dimension named above; an argument that names none is the same for every part. Nothing has to cross between parts.
Inputs may be any that keep to these rules, and one draw needn't show every extreme that they name: `tile_slot`: A permutation of 0 to 15.
All inputs are finite; a program needn't handle non-finite values.
Results may differ from a plain program's by a relative error of at most 0.02.
Values may be sent and summed in bfloat16 or wider, within the bound.
A program may use at most 128 MiB of HBM per device.

v0:
```python
import math

import jax
import jax.numpy as jnp
from jax import lax
from jax.sharding import PartitionSpec as P

TILE = 64


EPSILON = 1e-06


def passed_along(block, axis, distance):
    devices = range(lax.axis_size(axis))
    route = [((i - distance) % len(devices), i) for i in devices]
    return lax.ppermute(block, axis, route)


def slot_lists(neighbours, tile_slot):
    tile_count = tile_slot.shape[0]
    numbering = jnp.arange(tile_count, dtype=jnp.int32)
    placed = (tile_slot[:, None] == numbering[None, :]).astype(jnp.int32)
    tile_of_slot = jnp.sum(placed * numbering[:, None], axis=0)
    chosen = (tile_of_slot[:, None] == numbering[None, :]).astype(jnp.int32)
    listed_tiles = jnp.sum(chosen[:, :, None] * neighbours[None, :, :], axis=1)
    key_valid = listed_tiles >= 0
    safe_tiles = jnp.maximum(listed_tiles, 0)
    matches = (safe_tiles[:, :, None] == numbering[None, None, :]).astype(jnp.int32)
    key_slots = jnp.sum(matches * tile_slot[None, None, :], axis=2)
    return (key_slots, key_valid)


def block_tiles(tile_count):
    return math.gcd(tile_count, max(1, 512 // TILE))


def unit_norm(values):
    spread = jnp.sqrt(jnp.mean(values * values, axis=-1, keepdims=True) + EPSILON)
    return (values / spread, spread)


def probabilities(query_block, key_rows, block_valid):
    scores = jnp.einsum(
        "aihd,ajhd->ahij", query_block, key_rows, preferred_element_type=jnp.float32
    ) * (1.0 / math.sqrt(query_block.shape[-1]))
    key_mask = jnp.repeat(block_valid, TILE, axis=1)
    scores = jnp.where(key_mask[:, None, None, :], scores, -jnp.inf)
    row_max = jnp.max(scores, axis=-1, keepdims=True)
    weights = jnp.exp(scores - row_max)
    return (weights / jnp.sum(weights, axis=-1, keepdims=True)).astype(jnp.bfloat16)


def gathered(tiles_array, block_slots):
    picked = tiles_array[block_slots]
    return picked.reshape(block_slots.shape[0], -1, tiles_array.shape[2], tiles_array.shape[3])


def attend_both(query_tiles, key_tiles, value_tiles, grad_tiles, key_slots, key_valid):
    tile_count = query_tiles.shape[0]
    span = block_tiles(tile_count)
    scale_factor = 1.0 / math.sqrt(query_tiles.shape[-1])
    empty_grad = jnp.zeros(query_tiles.shape, jnp.float32)

    def per_block(accumulators, block_index):
        key_total, value_total = accumulators
        first_tile = block_index * span
        query_block = lax.dynamic_slice_in_dim(query_tiles, first_tile, span, 0)
        grad_block = lax.dynamic_slice_in_dim(grad_tiles, first_tile, span, 0)
        block_slots = lax.dynamic_slice_in_dim(key_slots, first_tile, span, 0)
        block_valid = lax.dynamic_slice_in_dim(key_valid, first_tile, span, 0)
        key_rows = gathered(key_tiles, block_slots)
        value_rows = gathered(value_tiles, block_slots)
        weights = probabilities(query_block, key_rows, block_valid)
        attended = jnp.einsum(
            "ahij,ajhd->aihd", weights, value_rows, preferred_element_type=jnp.float32
        )
        value_part = jnp.einsum(
            "ahij,aihd->ajhd", weights, grad_block, preferred_element_type=jnp.float32
        )
        prob_grad = jnp.einsum(
            "aihd,ajhd->ahij", grad_block, value_rows, preferred_element_type=jnp.float32
        )
        weights_wide = weights.astype(jnp.float32)
        row_delta = jnp.sum(weights_wide * prob_grad, axis=-1, keepdims=True)
        score_grad = (weights_wide * (prob_grad - row_delta) * scale_factor).astype(jnp.bfloat16)
        query_part = jnp.einsum(
            "ahij,ajhd->aihd", score_grad, key_rows, preferred_element_type=jnp.float32
        )
        key_part = jnp.einsum(
            "ahij,aihd->ajhd", score_grad, query_block, preferred_element_type=jnp.float32
        )
        block_shape = (span, block_slots.shape[1]) + query_tiles.shape[1:]
        key_total = key_total.at[block_slots].add(key_part.reshape(block_shape))
        value_total = value_total.at[block_slots].add(value_part.reshape(block_shape))
        return ((key_total, value_total), (attended, query_part))

    totals, parts = lax.scan(
        per_block, (empty_grad, empty_grad), jnp.arange(tile_count // span, dtype=jnp.int32)
    )
    flat_shape = (-1,) + query_tiles.shape[2:]
    return (
        parts[0].reshape(flat_shape),
        parts[1].reshape(flat_shape),
        totals[0].reshape(flat_shape),
        totals[1].reshape(flat_shape),
    )


def body(
    segment_input,
    output_grad,
    qkv_weight,
    out_weight,
    query_gain,
    key_gain,
    gate_scale,
    neighbours,
    tile_slot,
):
    key_slots, key_valid = slot_lists(neighbours, tile_slot)
    stream = segment_input[0]
    upstream = output_grad[0]
    model_width = stream.shape[1]
    head_dim = query_gain.shape[1]
    local_heads = qkv_weight.shape[2]
    local_width = local_heads * head_dim
    proj_weight = qkv_weight[0].reshape(model_width, local_heads * 3 * head_dim)
    out_local = out_weight[0]
    gate_row = gate_scale[0]
    query_weights = query_gain[0]
    key_weights = key_gain[0]
    projected = jnp.dot(
        lax.all_gather(stream, "seq", axis=0, tiled=True),
        proj_weight,
        preferred_element_type=jnp.float32,
    )
    all_tokens = projected.shape[0]
    projected = projected.reshape(all_tokens, local_heads, 3, head_dim)
    query_unit, query_spread = unit_norm(projected[:, :, 0])
    key_unit, key_spread = unit_norm(projected[:, :, 1])
    queries = (query_unit * query_weights).astype(jnp.bfloat16)
    keys_normed = (key_unit * key_weights).astype(jnp.bfloat16)
    value_rows = projected[:, :, 2].astype(jnp.bfloat16)
    scaled = (upstream.astype(jnp.float32) * gate_row).astype(jnp.bfloat16)
    attended_grad = jnp.einsum(
        "td,cd->tc",
        lax.all_gather(scaled, "seq", axis=0, tiled=True),
        out_local,
        preferred_element_type=jnp.float32,
    ).astype(jnp.bfloat16)

    def as_tiles(values):
        return values.reshape(-1, TILE, local_heads, head_dim)

    attended, query_grad, key_grad, value_grad = attend_both(
        as_tiles(queries),
        as_tiles(keys_normed),
        as_tiles(value_rows),
        as_tiles(attended_grad),
        key_slots,
        key_valid,
    )
    attended_low = attended.astype(jnp.bfloat16).reshape(all_tokens, local_width)
    rows = attended_low
    attention_out = lax.psum_scatter(
        jnp.dot(rows, out_local, preferred_element_type=jnp.float32),
        "seq",
        scatter_dimension=0,
        tiled=True,
    )
    section_out = (stream.astype(jnp.float32) + gate_row * attention_out).astype(jnp.bfloat16)
    segment_output = passed_along(section_out, "pipe", 1)
    gate_local = lax.psum_scatter(
        jnp.sum(upstream.astype(jnp.float32) * attention_out, axis=0),
        "seq",
        scatter_dimension=0,
        tiled=True,
    )
    query_scaled = query_grad * query_weights
    query_part_grad = (
        query_scaled - query_unit * jnp.mean(query_scaled * query_unit, axis=-1, keepdims=True)
    ) / query_spread
    key_scaled = key_grad * key_weights
    key_part_grad = (
        key_scaled - key_unit * jnp.mean(key_scaled * key_unit, axis=-1, keepdims=True)
    ) / key_spread
    projected_grad = (
        jnp.stack([query_part_grad, key_part_grad, value_grad], axis=2)
        .astype(jnp.bfloat16)
        .reshape(all_tokens, local_heads * 3 * head_dim)
    )
    rows = projected_grad
    stream_grad = lax.psum_scatter(
        jnp.einsum("tc,dc->td", rows, proj_weight, preferred_element_type=jnp.float32).astype(
            jnp.bfloat16
        ),
        "seq",
        scatter_dimension=0,
        tiled=True,
    ).astype(jnp.float32)
    token_grad = (upstream.astype(jnp.float32) + stream_grad).astype(jnp.bfloat16)
    input_grad = passed_along(token_grad, "pipe", -1)
    return (segment_output[None], input_grad[None], gate_local[None])


def solution(mesh):
    in_specs = (
        P("pipe", ("dp", "seq"), None),
        P("pipe", ("dp", "seq"), None),
        P("pipe", None, "seq", None),
        P("pipe", "seq", None),
        P("pipe", None),
        P("pipe", None),
        P("pipe", None),
        P("dp", None),
        P("dp"),
    )
    out_specs = (
        P("pipe", ("dp", "seq"), None),
        P("pipe", ("dp", "seq"), None),
        P(("dp", "pipe"), "seq"),
    )
    return jax.shard_map(body, mesh=mesh, in_specs=in_specs, out_specs=out_specs, check_vma=False)
```

profile of v0, /device:TPU:8, one launch (start us, length us, event | category | flops | bytes accessed | tf_op | source)
XLA Modules:
  0.0 508.9 jit_solution(14000528992266416604)
XLA Ops:
  8.0 1.8 fusion.46
  9.9 2.8 copy.22
  13.2 45.7 %all-gather.6.cloned.1.call-done = bf16[1,1024,3072]{2,1,0:T(8,128)(2,1)} async-done(((bf16[1,64,3072]{2,1,0:T(8,128)(2,1)}), bf16[1,1024,3072]{2,1,0:T(8,128)(2,1)}) %all-gather.6.cloned.1.call-update) | async-done | bytes 6291472 | tf_op jit(solution)/shard_map/all_gather | solution.py:134
  58.8 5.5 %fusion.43 = f32[1024,1,3,128]{3,0,2,1:T(8,128)S(1)} fusion(bf16[3,128,3072]{2,1,0:T(8,128)(2,1)S(1)} %bitcast.180, bf16[1,1024,3072]{2,1,0:T(8,128)(2,1)} %all-gather.6.cloned.1.call-done), kind=kOutput, calls=%fused_computation.52 | convolution fusion | flops 2415919104 | bytes 10223616 | tf_op jit(solution)/shard_map/dot_general | solution.py:133
  64.4 1.1 copy-done.6
  65.9 0.8 sqrt.32
  67.3 38.6 %all-gather.4.cloned.1.call-done = bf16[1024,3072]{1,0:T(8,128)(2,1)} async-done(((bf16[64,3072]{1,0:T(8,128)(2,1)}), bf16[1024,3072]{1,0:T(8,128)(2,1)}) %all-gather.4.cloned.1.call-update) | async-done | bytes 6291472 | tf_op jit(solution)/shard_map/all_gather | solution.py:148
  105.9 4.6 convolution_convert_fusion.1
  110.7 179.3 %while.16 = (s32[]{:T(128)}, f32[16,64,1,128]{3,1,0,2:T(8,128)S(1)}, f32[16,64,1,128]{3,1,0,2:T(8,128)S(1)}, bf16[2,8,64,1,128]{4,2,1,3,0:T(8,128)(2,1)}, f32[2,...) while((s32[]{:T(128)}, ...), condition=%wide.region_11.12_spmd, body=%wide.region_5.11_spmd.sunk | while | flops 1380196096 | bytes 147397712 | solution.py:98
  112.5 2.9 gather_fusion.1
  115.4 2.9 gather_fusion
  118.3 5.3 %exponential_reduce_fusion.2 = (f32[8,64]{1,0:T(8,128)S(1)}, f32[8,64,1728]{2,1,0:T(8,128)}) fusion(bf16[8,1728,128]{2,1,0:T(8,128)(2,1)} %bitcast.173, pred[8,1728]{1,0:T(8,128)(4,1)S(1)} %broadcast_in_dim.84, bf16[16,64,1,128]{3,1,0,2:T(8,128)(2,1)S(1)} %get-tuple-element.237, s32[]{:T(128)S(6)} %select_n.30), kind=kOutput, calls=%fused_computation.13.clone.1 | convolution fusion | flops 230033088 | bytes 7225348 | tf_op jit(solution)/shard_map/while/body/eval_jaxpr/sub | solution.py:50
  123.7 2.8 divide_convert_fusion.3
  126.4 1.2 copy-done.2
  127.7 0.9 fusion.97
  128.6 0.7 copy-done.10
  129.2 3.2 fusion.94
  132.5 7.1 %fusion.98 = f32[2,8,64,1,128]{4,2,1,3,0:T(8,128)} fusion(f32[2,8,64,1,128]{4,2,1,3,0:T(8,128)} %get-tuple-element.218, s32[]{:T(128)S(6)} %copy.34, bf16[8,1728,128]{2,1,0:T(8,128)(2,1)} %bitcast.174, bf16[8,64,1728]{2,1,0:T(8,128)(2,1)} %copy-done.2, f32[8,64,1728]{2,1,0:T(8,128)} %fusion.94), kind=kOutput, calls=%fused_computation.20.clone.1 | convolution fusion | flops 232687808 | bytes 14811140 | tf_op jit(solution)/shard_map/while/body/eval_jaxpr/ahij,ajhd->aihd/dot_general | solution.py:87
  139.6 8.8 %fusion.95 = f32[8,128,1728]{1,2,0:T(8,128)} fusion(bf16[8,64,1728]{2,1,0:T(8,128)(2,1)} %copy-done.2, f32[8,64,1728]{2,1,0:T(8,128)} %fusion.94, bf16[16,64,1,128]{3,1,0,2:T(8,128)(2,1)S(1)} %get-tuple-element.237, s32[]{:T(128)S(6)} %select_n.30), kind=kOutput, calls=%fused_computation.16.clone.1 | convolution fusion | flops 232687808 | bytes 18219012 | tf_op jit(solution)/shard_map/while/body/eval_jaxpr/ahij,aihd->ajhd/dot_general | solution.py:90
  148.3 23.2 %scatter_fusion = f32[16,64,128]{2,1,0:T(8,128)S(1)} fusion(f32[16,64,128]{2,1,0:T(8,128)S(1)} %bitcast.162, s32[216]{0:T(256)S(1)} %reshape.617, f32[216,64,128]{2,1,0:T(8,128)} %bitcast.172), kind=kCustom, calls=%fused_computation.2.clone.1 | custom fusion | flops 1769472 | bytes 21234528 | tf_op jit(solution)/shard_map/while/body/eval_jaxpr/scatter-add | solution.py:94
  171.6 5.7 %fusion.96 = f32[8,128,1728]{1,2,0:T(8,128)} fusion(bf16[8,64,1728]{2,1,0:T(8,128)(2,1)} %copy-done.2, bf16[16,64,1,128]{3,1,0,2:T(8,128)(2,1)S(1)} %get-tuple-element.240, s32[]{:T(128)S(6)} %select_n.30), kind=kOutput, calls=%fused_computation.23.clone.1 | convolution fusion | flops 226492416 | bytes 8978436 | tf_op jit(solution)/shard_map/while/body/eval_jaxpr/ahij,aihd->ajhd/dot_general | solution.py:78
  177.2 23.2 %scatter_fusion.1 = f32[16,64,128]{2,1,0:T(8,128)S(1)} fusion(f32[16,64,128]{2,1,0:T(8,128)S(1)} %bitcast.164, s32[216]{0:T(256)S(1)} %reshape.617, f32[216,64,128]{2,1,0:T(8,128)} %bitcast.171), kind=kCustom, calls=%fused_computation.3.clone.1 | custom fusion | flops 1769472 | bytes 21234528 | tf_op jit(solution)/shard_map/while/body/eval_jaxpr/scatter-add | solution.py:95
  202.1 2.9 gather_fusion.1
  205.0 2.9 gather_fusion
  207.9 5.3 %exponential_reduce_fusion.2 = (f32[8,64]{1,0:T(8,128)S(1)}, f32[8,64,1728]{2,1,0:T(8,128)}) fusion(bf16[8,1728,128]{2,1,0:T(8,128)(2,1)} %bitcast.173, pred[8,1728]{1,0:T(8,128)(4,1)S(1)} %broadcast_in_dim.84, bf16[16,64,1,128]{3,1,0,2:T(8,128)(2,1)S(1)} %get-tuple-element.237, s32[]{:T(128)S(6)} %select_n.30), kind=kOutput, calls=%fused_computation.13.clone.1 | convolution fusion | flops 230033088 | bytes 7225348 | tf_op jit(solution)/shard_map/while/body/eval_jaxpr/sub | solution.py:50
  213.2 2.8 divide_convert_fusion.3
  216.0 1.2 copy-done.2
  217.3 0.9 fusion.97
  218.1 0.7 copy-done.10
  218.8 3.2 fusion.94
  222.0 7.1 %fusion.98 = f32[2,8,64,1,128]{4,2,1,3,0:T(8,128)} fusion(f32[2,8,64,1,128]{4,2,1,3,0:T(8,128)} %get-tuple-element.218, s32[]{:T(128)S(6)} %copy.34, bf16[8,1728,128]{2,1,0:T(8,128)(2,1)} %bitcast.174, bf16[8,64,1728]{2,1,0:T(8,128)(2,1)} %copy-done.2, f32[8,64,1728]{2,1,0:T(8,128)} %fusion.94), kind=kOutput, calls=%fused_computation.20.clone.1 | convolution fusion | flops 232687808 | bytes 14811140 | tf_op jit(solution)/shard_map/while/body/eval_jaxpr/ahij,ajhd->aihd/dot_general | solution.py:87
  229.2 8.8 %fusion.95 = f32[8,128,1728]{1,2,0:T(8,128)} fusion(bf16[8,64,1728]{2,1,0:T(8,128)(2,1)} %copy-done.2, f32[8,64,1728]{2,1,0:T(8,128)} %fusion.94, bf16[16,64,1,128]{3,1,0,2:T(8,128)(2,1)S(1)} %get-tuple-element.237, s32[]{:T(128)S(6)} %select_n.30), kind=kOutput, calls=%fused_computation.16.clone.1 | convolution fusion | flops 232687808 | bytes 18219012 | tf_op jit(solution)/shard_map/while/body/eval_jaxpr/ahij,aihd->ajhd/dot_general | solution.py:90
  237.9 23.2 %scatter_fusion = f32[16,64,128]{2,1,0:T(8,128)S(1)} fusion(f32[16,64,128]{2,1,0:T(8,128)S(1)} %bitcast.162, s32[216]{0:T(256)S(1)} %reshape.617, f32[216,64,128]{2,1,0:T(8,128)} %bitcast.172), kind=kCustom, calls=%fused_computation.2.clone.1 | custom fusion | flops 1769472 | bytes 21234528 | tf_op jit(solution)/shard_map/while/body/eval_jaxpr/scatter-add | solution.py:94
  261.2 5.7 %fusion.96 = f32[8,128,1728]{1,2,0:T(8,128)} fusion(bf16[8,64,1728]{2,1,0:T(8,128)(2,1)} %copy-done.2, bf16[16,64,1,128]{3,1,0,2:T(8,128)(2,1)S(1)} %get-tuple-element.240, s32[]{:T(128)S(6)} %select_n.30), kind=kOutput, calls=%fused_computation.23.clone.1 | convolution fusion | flops 226492416 | bytes 8978436 | tf_op jit(solution)/shard_map/while/body/eval_jaxpr/ahij,aihd->ajhd/dot_general | solution.py:78
  266.8 23.2 %scatter_fusion.1 = f32[16,64,128]{2,1,0:T(8,128)S(1)} fusion(f32[16,64,128]{2,1,0:T(8,128)S(1)} %bitcast.164, s32[216]{0:T(256)S(1)} %reshape.617, f32[216,64,128]{2,1,0:T(8,128)} %bitcast.171), kind=kCustom, calls=%fused_computation.3.clone.1 | custom fusion | flops 1769472 | bytes 21234528 | tf_op jit(solution)/shard_map/while/body/eval_jaxpr/scatter-add | solution.py:95
  290.1 1.4 multiply_reduce_fusion
  291.6 1.4 multiply_reduce_fusion.1
  293.2 2.2 divide_convert_fusion.1
  295.8 7.1 %convolution_convert_fusion = bf16[1024,3072]{1,0:T(8,128)(2,1)} fusion(bf16[1024,384]{0,1:T(8,128)(2,1)S(1)} %bitcast.183, bf16[1,3072,1,384]{3,1,2,0:T(8,128)(2,1)} %param.13), kind=kOutput, calls=%fused_computation.50 | convolution fusion | flops 2419064832 | bytes 9437184 | tf_op jit(solution)/shard_map/tc,dc->td/dot_general | solution.py:195
  303.0 0.9 copy-done.11
  303.9 6.4 %fusion.50 = f32[1024,3072]{1,0:T(8,128)} fusion(bf16[1024,128]{1,0:T(8,128)(2,1)S(1)} %bitcast.186, bf16[1,128,3072]{2,1,0:T(8,128)(2,1)S(1)} %copy-done), kind=kOutput, calls=%fused_computation.63 | convolution fusion | flops 805306368 | bytes 13631488 | tf_op jit(solution)/shard_map/dot_general | solution.py:167
  310.3 58.0 %reduce-scatter.5.cloned.1.call-done = bf16[64,3072]{1,0:T(8,128)(2,1)} async-done(((bf16[1024,3072]{1,0:T(8,128)(2,1)}), bf16[64,3072]{1,0:T(8,128)(2,1)}) %reduce-scatter.5.cloned.1.call-update) | async-done | bytes 393232 | tf_op jit(solution)/shard_map/reduce_scatter | solution.py:194
  368.2 80.7 %reduce-scatter.3.cloned.1.call-done = f32[64,3072]{1,0:T(8,128)} async-done(((f32[1024,3072]{1,0:T(8,128)}), f32[64,3072]{1,0:T(8,128)}) %reduce-scatter.3.cloned.1.call-update) | async-done | bytes 786448 | tf_op jit(solution)/shard_map/reduce_scatter | solution.py:166
  449.0 1.5 fusion.48
  450.5 1.6 collective-permute-start
  453.8 46.4 %all-reduce = f32[3072]{0:T(1024)S(1)} all-reduce(f32[3072]{0:T(1024)S(1)} %get-tuple-element.116), channel_id=5, replica_groups=mesh['seq'=16,'pipe'=4,'dp'=4] {'seq'}, use_global_device_ids=true, to_apply=%region_17.18.clone | all-reduce | flops 3072 | bytes 24576
  500.8 0.7 copy.46
  501.6 0.7 copy.47
  (108 shorter events, 6.6 us)
Async XLA Ops:
  7.2 98.8 %copy-start = (bf16[1,128,3072]{2,1,0:T(8,128)(2,1)S(1)}, bf16[1,128,3072]{2,1,0:T(8,128)(2,1)}, u32[]{:S(2)}) copy-start(bf16[1,128,3072]{2,1,0:T(8,128)(2,1)} %param.14) | copy-start | bytes 2359300
  7.2 5.6 %copy-start.25 = (s32[16]{0:T(128)S(1)}, s32[16]{0:T(128)}, u32[]{:S(2)}) copy-start(s32[16]{0:T(128)} %param.19) | copy-start | bytes 196
  7.2 5.7 %copy-start.20 = (s32[16,27]{1,0:T(8,128)S(1)}, s32[16,27]{1,0:T(8,128)}, u32[]{:S(2)}) copy-start(s32[16,27]{1,0:T(8,128)} %param.18) | copy-start | bytes 5188
  7.2 51.6 %all-gather.6.cloned.1.call-start = ((), (), s32[]{:S(2)}) async-start(), calls=%async_computation.5 | async-start | bytes 6684672 | tf_op jit(solution)/shard_map/all_gather | solution.py:134
  7.9 98.0 %all-gather.4.cloned.1.call-start = ((), (), s32[]{:S(2)}) async-start(), calls=%async_computation.2 | async-start | bytes 6684672 | tf_op jit(solution)/shard_map/all_gather | solution.py:148
  9.8 358.4 %reduce-scatter.5.cloned.1.call-start = ((), (), s32[]{:S(2)}) async-start(), calls=%async_computation.4 | async-start | bytes 6684672 | tf_op jit(solution)/shard_map/reduce_scatter | solution.py:194
  58.8 8.1 %copy-start.21 = (f32[1,128]{1,0:T(1,128)S(1)}, f32[1,128]{1,0:T(1,128)}, u32[]{:S(2)}) copy-start(f32[1,128]{1,0:T(1,128)} %param.15) | copy-start | bytes 1540
  58.8 8.3 %copy-start.23 = (f32[1,128]{1,0:T(1,128)S(1)}, f32[1,128]{1,0:T(1,128)}, u32[]{:S(2)}) copy-start(f32[1,128]{1,0:T(1,128)} %param.16) | copy-start | bytes 1540
  64.4 1.2 copy-start.6
  65.9 44.6 %copy-start.3 = (f32[1024,1,1,128]{3,0,2,1:T(8,128)}, f32[1024,1,1,128]{3,0,2,1:T(8,128)S(1)}, u32[]{:S(2)}) copy-start(f32[1024,1,1,128]{3,0,2,1:T(8,128)S(1)} %get-tuple-element.115) | copy-start | bytes 1572868
  65.9 44.6 %copy-start.5 = (f32[1024,1,1,128]{3,0,2,1:T(8,128)}, f32[1024,1,1,128]{3,0,2,1:T(8,128)S(1)}, u32[]{:S(2)}) copy-start(f32[1024,1,1,128]{3,0,2,1:T(8,128)S(1)} %get-tuple-element.114) | copy-start | bytes 1572868
  65.9 1.2 copy-start.14
  65.9 44.6 %copy-start.17 = (f32[1024]{0:T(1024)}, f32[1024]{0:T(1024)S(1)}, u32[]{:S(2)}) copy-start(f32[1024]{0:T(1024)S(1)} %get-tuple-element.119) | copy-start | bytes 12292
  66.9 43.6 %copy-start.12 = (f32[16,64]{1,0:T(8,128)}, f32[16,64]{1,0:T(8,128)S(1)}, u32[]{:S(2)}) copy-start(f32[16,64]{1,0:T(8,128)S(1)} %sqrt.31) | copy-start | bytes 12292
  110.7 179.4 %copy-start.13 = (f32[16,64]{1,0:T(8,128)S(1)}, f32[16,64]{1,0:T(8,128)}, u32[]{:S(2)}) copy-start(f32[16,64]{1,0:T(8,128)} %copy-done.12) | copy-start | bytes 12292
  110.7 179.4 %copy-start.24 = (f32[1,128]{1,0:T(1,128)S(1)}, f32[1,128]{1,0:T(1,128)}, u32[]{:S(2)}) copy-start(f32[1,128]{1,0:T(1,128)} %param.16) | copy-start | bytes 1540
  110.7 180.9 %copy-start.4 = (f32[1024,1,1,128]{3,0,2,1:T(8,128)S(1)}, f32[1024,1,1,128]{3,0,2,1:T(8,128)}, u32[]{:S(2)}) copy-start(f32[1024,1,1,128]{3,0,2,1:T(8,128)} %copy-done.3) | copy-start | bytes 1572868
  110.7 180.9 %copy-start.19 = (f32[2,8,64]{2,1,0:T(8,128)S(1)}, f32[2,8,64]{2,1,0:T(8,128)}, u32[]{:S(2)}) copy-start(f32[2,8,64]{2,1,0:T(8,128)} %sqrt.32) | copy-start | bytes 12292
  110.7 180.9 %copy-start.22 = (f32[1,128]{1,0:T(1,128)S(1)}, f32[1,128]{1,0:T(1,128)}, u32[]{:S(2)}) copy-start(f32[1,128]{1,0:T(1,128)} %param.15) | copy-start | bytes 1540
  110.7 182.5 %copy-start.15 = (f32[1024]{0:T(1024)S(1)}, f32[1024]{0:T(1024)}, u32[]{:S(2)}) copy-start(f32[1024]{0:T(1024)} %copy-done.14) | copy-start | bytes 12292
  110.7 182.5 %copy-start.18 = (f32[1024]{0:T(1024)S(1)}, f32[1024]{0:T(1024)}, u32[]{:S(2)}) copy-start(f32[1024]{0:T(1024)} %copy-done.17) | copy-start | bytes 12292
  123.6 4.0 copy-start.1
  123.6 4.0 copy-start.9
  126.4 1.2 copy-start.2
  128.5 0.7 copy-start.10
  213.2 4.0 copy-start.1
  213.2 4.0 copy-start.9
  216.0 1.2 copy-start.2
  218.1 0.7 copy-start.10
  302.9 0.9 copy-start.11
  302.9 146.0 %reduce-scatter.3.cloned.1.call-start = ((), (), s32[]{:S(2)}) async-start(), calls=%async_computation.3 | async-start | bytes 13369344 | tf_op jit(solution)/shard_map/reduce_scatter | solution.py:166
  310.2 138.7 %copy-start.7 = (bf16[1,64,3072]{2,1,0:T(8,128)(2,1)S(1)}, bf16[1,64,3072]{2,1,0:T(8,128)(2,1)}, u32[]{:S(2)}) copy-start(bf16[1,64,3072]{2,1,0:T(8,128)(2,1)} %param.11) | copy-start | bytes 1179652
  310.2 138.7 %copy-start.8 = (bf16[1,64,3072]{2,1,0:T(8,128)(2,1)S(1)}, bf16[1,64,3072]{2,1,0:T(8,128)(2,1)}, u32[]{:S(2)}) copy-start(bf16[1,64,3072]{2,1,0:T(8,128)(2,1)} %param.12) | copy-start | bytes 1179652
  310.2 138.7 %copy-start.16 = (f32[1,3072]{1,0:T(1,128)S(1)}, f32[1,3072]{1,0:T(1,128)}, u32[]{:S(2)}) copy-start(f32[1,3072]{1,0:T(1,128)} %param.17) | copy-start | bytes 36868
  310.2 142.3 %copy-start.26 = (u32[256]{0:T(256)S(1)}, u32[256]{0:T(256)}, u32[]{:S(2)}) copy-start(u32[256]{0:T(256)} %constant.48) | copy-start | bytes 3076
  450.5 50.4 %collective-permute-start = (bf16[64,3072]{1,0:T(8,128)(2,1)S(1)}, bf16[64,3072]{1,0:T(8,128)(2,1)S(1)}, u32[]{:S(2)}, u32[]{:S(2)}) collective-permute-start(bf16[64,3072]{1,0:T(8,128)(2,1)S(1)} %get-tuple-element.117), channel_id=1, source_target_pairs={{12,0},{0,4},{4,8},{8,12},{13,1},{1,5},{5,9},{9,13},{14,2},{2,6},{... | collective-permute-start | bytes 1179656 | tf_op jit(solution)/shard_map/ppermute | solution.py:17
  452.0 48.8 %collective-permute-start.1 = (bf16[64,3072]{1,0:T(8,128)(2,1)S(1)}, bf16[64,3072]{1,0:T(8,128)(2,1)S(1)}, u32[]{:S(2)}, u32[]{:S(2)}) collective-permute-start(bf16[64,3072]{1,0:T(8,128)(2,1)S(1)} %get-tuple-element.118), channel_id=1, source_target_pairs={{4,0},{8,4},{12,8},{0,12},{5,1},{9,5},{13,9},{1,13},{6,2},{10,6},{... | collective-permute-start | bytes 1179656 | tf_op jit(solution)/shard_map/ppermute | solution.py:17
Sparse Core Ops, SparseCore 0:
  9.9 48.9 all-gather.5
  61.2 44.6 all-gather.3
  303.1 65.0 reduce-scatter.4
  370.6 78.2 reduce-scatter.2
where the time goes:
time: 514 us; the launch traced here: 509 us
  waiting for transfers between devices  224 us (44%)
  other arithmetic  108 us (21%)
  matrix products  85.4 us (17%)
  blocking collectives  46.4 us (9%)
  local copies, waits for them, and re-layouts  26.4 us (5%)
  between operations  14.8 us (3%)
    reduce_scatter x1, waiting for transfers between devices, body(): lax.psum_scatter(jnp.dot(rows, out_local, preferred_element_type=jnp.floa...  80.7 us
    reduce_scatter x1, waiting for transfers between devices, body(): lax.psum_scatter(jnp.einsum('tc,dc->td', rows, proj_weight, preferred_ele...  58 us
    scatter-add x2, other arithmetic, per_block(): value_total.at[block_slots].add(value_part.reshape(block_shape))  46.5 us
    scatter-add x2, other arithmetic, per_block(): key_total = key_total.at[block_slots].add(key_part.reshape(block_shape))  46.5 us
    unnamed x1, blocking collectives  46.4 us
    all_gather x1, waiting for transfers between devices, body(): lax.all_gather(stream, 'seq', axis=0, tiled=True)  45.7 us
    all_gather x1, waiting for transfers between devices, body(): lax.all_gather(scaled, 'seq', axis=0, tiled=True)  38.6 us
    dot_general x2, matrix products, per_block(): jnp.einsum('ahij,aihd->ajhd', score_grad, query_block, preferred_element_...  17.5 us
  transfers between devices with their start and end apart: 6, of which 4 were waited for; matrix products, arithmetic and copies ran while one was open for 4% of the time, Pallas kernels for 0%

commit v1 on v0

v1 whole, which is shorter than its diff:
```python
import functools
import math

import jax
import jax.numpy as jnp
from jax import lax
from jax.experimental import pallas as pl
from jax.experimental.pallas import tpu as pltpu
from jax.sharding import PartitionSpec as P

EPSILON = 1e-06
MESH = pl.DeviceIdType.MESH
F32 = jnp.float32
BF16 = jnp.bfloat16
D = 3072
HD = 128
TILE = 64
NZ = 8
COLS = 512
NT = (((1,), (1,)), ((), ()))


def dot(a, b):
    return jnp.dot(a, b, preferred_element_type=F32)


def dot_nt(a, b):
    return lax.dot_general(a, b, NT, preferred_element_type=F32)


def kernel(
    stream, upstream, wqkv, wout, qgain, kgain, gate, neigh, tslot,
    fwd_out, bwd_out, gate_out,
    Sg, UP, SC, WQ, WO, PJX, PJ1, BIAS, Qb, Kb, Vb, KT, VT, Pb, ATT, AH, DOS, DO,
    dQ, dK, dV, PGO, PGX, PGP, GT, SB, RB, AOUT, AOX, FO, BO, GS, GR,
    ld, zs_s, zs_r, zw_s, zw_r, xw_s, xw_r, pj_s, pj_r, ex_s, ex_r,
    at_s, at_r, do_s, do_r, rs_s, rs_r, y_s, y_r, g_s, g_r,
):
    seq = lax.axis_index("seq")
    x = lax.axis_index("dp")
    y = lax.axis_index("pipe")
    z = lax.div(seq, 2)
    c = lax.rem(seq, 2)

    def dev(d, e=0):
        return {"seq": 2 * lax.rem(z + d, NZ) + (c if e == 0 else 1 - c)}

    right, left, partner = dev(1), dev(NZ - 1), dev(0, 1)
    xr = {"dp": lax.rem(x + 1, 4)}
    xl = {"dp": lax.rem(x + 3, 4)}
    yn = {"pipe": lax.rem(y + 1, 4)}
    yp = {"pipe": lax.rem(y + 3, 4)}

    sent = []

    def remote(src, dst, ssem, rsem, to):
        return pltpu.make_async_remote_copy(
            src_ref=src, dst_ref=dst, send_sem=ssem, recv_sem=rsem,
            device_id=to, device_id_type=MESH)

    def go(copy):
        copy.start()
        sent.append(copy)

    loads = [
        pltpu.make_async_copy(wout, WO.at[0], ld.at[0]),
        pltpu.make_async_copy(stream, Sg.at[0], ld.at[1]),
        pltpu.make_async_copy(upstream, UP.at[0], ld.at[2]),
        pltpu.make_async_copy(wqkv, WQ.at[0], ld.at[3]),
    ]
    for copy in loads:
        copy.start()

    barrier = pltpu.get_barrier_semaphore()
    peers = [dev(d, e) for d in range(NZ) for e in range(2) if d or e] + [xr, xl, yn, yp]
    for peer in peers:
        pl.semaphore_signal(barrier, inc=1, device_id=peer, device_id_type=MESH)
    pl.semaphore_wait(barrier, len(peers))

    def at(way, j):
        return (NZ - j) % NZ if way == 0 else j % NZ

    def ring_to(way):
        return right if way == 0 else left

    def s_unit(way, k):
        j, half = k // 2, (k + way) % 2
        return remote(Sg.at[at(way, j), half], Sg.at[at(way, j + 1), half],
                      zs_s.at[way, k], zs_r.at[way, k], ring_to(way))

    def w_unit(way, m):
        src, dst = WO.at[at(way, m), x], WO.at[at(way, m + 1), x]
        if m == 3:
            src, dst = src.at[way], dst.at[way]
        return remote(src, dst, zw_s.at[way, m], zw_r.at[way, m], ring_to(way))

    def x_unit(d, kind):
        quarter = [x, x, lax.rem(x + 3, 4), lax.rem(x + 1, 4)][kind]
        ref = WO.at[d, quarter]
        if kind >= 2:
            ref = ref.at[kind - 2]
        return remote(ref, ref, xw_s.at[d, kind], xw_r.at[d, kind], xr if kind % 2 == 0 else xl)

    def s_wait(k):
        for way in (0, 1):
            s_unit(way, k).wait_recv()

    def s_next(k):
        s_wait(k)
        if k + 2 <= 6:
            for way in (0, 1):
                go(s_unit(way, k + 2))

    def w_next(m):
        for way in (0, 1):
            w_unit(way, m).wait_recv()
            if m + 1 <= 3:
                go(w_unit(way, m + 1))

    def x_send(d):
        go(x_unit(d, 0))
        go(x_unit(d, 1))

    def x_next(d):
        x_unit(d, 0).wait_recv()
        go(x_unit(d, 2))
        x_unit(d, 1).wait_recv()
        go(x_unit(d, 3))

    def x_done(d):
        x_unit(d, 2).wait_recv()
        x_unit(d, 3).wait_recv()

    def project(ds):
        rows = [Sg.at[d] for d in ds]

        def one(e, carry):
            lhs = [r[...].reshape(TILE, D) for r in rows]
            lhs = lhs[0] if len(lhs) == 1 else jnp.concatenate(lhs, axis=0)
            out = dot(lhs, WQ[e])
            for n, d in enumerate(ds):
                PJX[e, d] = out[n * TILE:(n + 1) * TILE]
            return carry

        lax.fori_loop(0, 2, one, 0)
        for d in ds:
            go(pj_unit(d))

    def pj_unit(d):
        return remote(PJX.at[1, d], PJ1.at[d], pj_s.at[d], pj_r.at[d], partner)

    def do_unit(d):
        return remote(DOS.at[d], DO.at[(NZ - d) % NZ], do_s.at[d], do_r.at[d], dev(d))

    def grads_in(ds):
        for d in ds:
            val = dot_nt(SC[...], WO[d].reshape(HD, D)).astype(BF16)
            if d == 0:
                DO[0] = val
            else:
                DOS[d] = val
                go(do_unit(d))

    up_x = remote(UP.at[0], UP.at[1], ex_s.at[0], ex_r.at[0], partner)
    wq_x = remote(WQ.at[0], WQ.at[1], ex_s.at[1], ex_r.at[1], partner)

    loads[0].wait()
    go(w_unit(0, 0))
    go(w_unit(1, 0))
    loads[1].wait()
    for k in (0, 1):
        for way in (0, 1):
            go(s_unit(way, k))
    loads[2].wait()
    go(up_x)
    loads[3].wait()
    go(wq_x)

    i_rows = lax.broadcasted_iota(jnp.int32, (16, 16), 0)
    rel_z = z + lax.div(i_rows, 2)
    rel_z = jnp.where(rel_z >= NZ, rel_z - NZ, rel_z)
    odd = lax.rem(i_rows, 2)
    rel_slot = 2 * rel_z + jnp.where(odd == 0, c, 1 - c)
    lanes16 = lax.broadcasted_iota(jnp.int32, (16, 16), 1)
    listed = jnp.zeros((16, 16), F32)
    for k in range(neigh.shape[1]):
        listed = listed + jnp.where(neigh[:, k:k + 1] == lanes16, 1.0, 0.0)
    holds = jnp.where(rel_slot == tslot[...], 1.0, 0.0)
    by_key = dot_nt(holds, listed)
    by_key = dot_nt(by_key, holds)
    spread = jnp.where(
        lax.div(lax.broadcasted_iota(jnp.int32, (16, 1024), 1), TILE)
        == lax.broadcasted_iota(jnp.int32, (16, 1024), 0), 1.0, 0.0)
    bias = jnp.where(dot(by_key, spread) > 0.5, 0.0, -jnp.inf)
    for d in range(NZ):
        BIAS[d] = bias[:, d * HD:(d + 1) * HD]

    w_next(0)
    x_send(7)
    x_send(1)
    up_x.wait_recv()
    SC[...] = (UP[...].astype(F32) * gate[...]).astype(BF16).reshape(2 * TILE, D)
    wq_x.wait_recv()
    project([0])
    s_next(0)
    x_next(7)
    s_next(1)
    grads_in([0])
    x_next(1)
    project([7, 1])
    w_next(1)
    x_send(6)
    x_send(2)
    s_next(2)
    x_next(6)
    x_done(7)
    x_done(1)
    grads_in([7, 1])
    s_next(3)
    x_next(2)
    project([6, 2])
    w_next(2)
    x_send(5)
    x_send(3)
    s_next(4)
    x_next(5)
    x_done(6)
    x_done(2)
    grads_in([6, 2])
    s_next(5)
    x_next(3)
    project([5, 3])
    w_next(3)
    x_send(4)
    s_next(6)
    project([4])
    x_done(5)
    x_done(3)
    grads_in([5, 3])
    x_next(4)

    for d in range(NZ):
        pj_unit(d).wait_recv()

    def both(d):
        return jnp.concatenate([PJX[0, d], PJ1[d]], axis=0)

    def unit_of(part):
        spread = jnp.sqrt(jnp.mean(part * part, axis=-1, keepdims=True) + EPSILON)
        return part / spread, spread

    def norm(d, carry):
        pj = both(d)
        q_unit, _ = unit_of(pj[:, :HD])
        k_unit, _ = unit_of(pj[:, HD:2 * HD])
        Qb[d] = (q_unit * qgain[...]).astype(BF16)
        k = k_unit * kgain[...]
        v = pj[:, 2 * HD:]
        Kb[d] = k.astype(BF16)
        Vb[d] = v.astype(BF16)
        cols = pl.ds(pl.multiple_of(d * HD, HD), HD)
        KT[:, cols] = k.T.astype(BF16)
        VT[:, cols] = v.T.astype(BF16)
        return carry

    lax.fori_loop(0, NZ, norm, 0)
    scale = 1.0 / math.sqrt(HD)

    def attend(d, carry):
        s = dot_nt(Kb[...].reshape(NZ * HD, HD), Qb[d]) * scale
        s = s.reshape(16, TILE, HD) + BIAS[d][:, None, :]
        s = s.reshape(NZ * HD, HD)
        p = jnp.exp(s - jnp.max(s, axis=0, keepdims=True))
        p = (p * (1.0 / jnp.sum(p, axis=0, keepdims=True))).astype(BF16)
        Pb[d] = p
        ATT[d] = dot(VT[...], p).T.astype(BF16)
        return carry

    lax.fori_loop(0, NZ, attend, 0)

    def at_unit(d):
        back = (NZ - d) % NZ
        return remote(ATT.at[d], AH.at[:, back * HD:(back + 1) * HD], at_s.at[d], at_r.at[d], dev(d))

    x_done(4)
    grads_in([4])
    for d in range(1, NZ):
        go(at_unit(d))
    AH[:, :HD] = ATT[0]
    dK[...] = jnp.zeros_like(dK)
    dV[...] = jnp.zeros_like(dV)
    for d in range(1, NZ):
        do_unit(d).wait_recv()

    def attend_back(d, carry):
        grad, p = DO[d], Pb[d]
        dV[...] += dot(p, grad)
        dp = dot_nt(Vb[...].reshape(NZ * HD, HD), grad)
        wide = p.astype(F32)
        delta = jnp.sum(wide * dp, axis=0, keepdims=True)
        ds = (wide * (dp - delta) * scale).astype(BF16)
        dK[...] += dot(ds, Qb[d])
        dQ[d] = dot(KT[...], ds).T
        return carry

    lax.fori_loop(0, NZ, attend_back, 0)

    def norm_back(d, carry):
        pj = both(d)
        rows = pl.ds(pl.multiple_of(d * HD, HD), HD)

        def one(part, grad, gain):
            unit, spread = unit_of(part)
            a = grad * gain
            return (a - unit * jnp.mean(a * unit, axis=-1, keepdims=True)) / spread

        gq = one(pj[:, :HD], dQ[d], qgain[...])
        gk = one(pj[:, HD:2 * HD], dK[rows, :], kgain[...])
        pg = jnp.concatenate([gq, gk, dV[rows, :]], axis=1).astype(BF16)
        PGO[d] = pg[:TILE]
        PGX[d] = pg[TILE:]
        return carry

    lax.fori_loop(0, NZ, norm_back, 0)
    pg_x = remote(PGX, PGP, ex_s.at[2], ex_r.at[2], partner)
    go(pg_x)
    pg_x.wait_recv()

    def group(ds):
        def pick(ref):
            parts = [ref[d] for d in ds]
            return parts[0] if len(parts) == 1 else jnp.concatenate(parts, axis=0)

        def one(n, carry):
            cols = pl.ds(pl.multiple_of(n * COLS, COLS), COLS)
            out = dot_nt(pick(PGO), WQ[0, cols, :]) + dot_nt(pick(PGP), WQ[1, cols, :])
            for i in range(len(ds)):
                GT[i, :, cols] = out[i * TILE:(i + 1) * TILE]
            return carry

        lax.fori_loop(0, D // COLS, one, 0)

    plan = [(4, 0, None), (3, 1, None), (3, 0, 0), (2, 1, 1), (2, 0, 2), (1, 1, 3), (1, 0, 4)]

    def rs_unit(way, k):
        return remote(SB.at[way, k], RB.at[way, k], rs_s.at[way, k], rs_r.at[way, k], ring_to(way))

    def rs_send(k, slot):
        _, half, needs = plan[k]
        for way in (0, 1):
            h = half if way == 0 else 1 - half
            i = slot[way]
            val = GT[i, h * 32:(h + 1) * 32, :]
            if needs is not None:
                rs_unit(way, needs).wait_recv()
                val = val + RB[way, needs].astype(F32)
            SB[way, k] = val.astype(BF16)
            go(rs_unit(way, k))

    group([4])
    rs_send(0, (0, 0))
    group([3, 5])
    rs_send(1, (0, 1))
    rs_send(2, (0, 1))
    group([2, 6])
    rs_send(3, (0, 1))
    rs_send(4, (0, 1))

    for d in range(1, NZ):
        at_unit(d).wait_recv()

    def out_proj(n, carry):
        cols = pl.ds(pl.multiple_of(n * COLS, COLS), COLS)
        w = WO[:, :, :, :, cols].reshape(NZ * HD, COLS)
        out = dot(AH[...], w)
        AOUT[0, :, cols] = out[:TILE]
        AOUT[1, :, cols] = out[TILE:]
        return carry

    lax.fori_loop(0, D // COLS, out_proj, 0)
    ao_x = remote(AOUT.at[1], AOX, ex_s.at[3], ex_r.at[3], partner)
    go(ao_x)
    group([1, 7])
    rs_send(5, (0, 1))
    rs_send(6, (0, 1))
    ao_x.wait_recv()
    wide_ao = AOUT[0] + AOX[...]
    FO[...] = (Sg[0].reshape(TILE, D).astype(F32) + gate[...] * wide_ao).astype(BF16)
    fo_y = remote(FO, fwd_out, y_s.at[0], y_r.at[0], yn)
    go(fo_y)
    gsum = jnp.sum((UP[0].astype(F32) * wide_ao).reshape(8, 8, D), axis=0)
    for n in range(16):
        GS[n] = gsum[:, n * 192:(n + 1) * 192]

    def g_unit(d, e):
        i = 2 * d + e
        own = dev(d, e)["seq"]
        return remote(GS.at[own], GR.at[2 * ((NZ - d) % NZ) + e], g_s.at[i], g_r.at[i], dev(d, e))

    pairs = [(d, e) for d in range(NZ) for e in range(2) if d or e]
    for d, e in pairs:
        go(g_unit(d, e))
    GR[0] = GS[seq]
    group([0])
    for d, e in pairs:
        g_unit(d, e).wait_recv()
    gate_out[...] = jnp.sum(jnp.sum(GR[...], axis=0), axis=0, keepdims=True)

    def bo_unit(h):
        return remote(BO.at[h], bwd_out.at[h], y_s.at[1 + h], y_r.at[1 + h], yp)

    for h in (1, 0):
        first, second = (5, 6) if h == 1 else (6, 5)
        rs_unit(0, first).wait_recv()
        rs_unit(1, second).wait_recv()
        total = GT[0, h * 32:(h + 1) * 32, :] + RB[0, first].astype(F32) + RB[1, second].astype(F32)
        BO[h] = (UP[0, h * 32:(h + 1) * 32, :].astype(F32) + total).astype(BF16)
        go(bo_unit(h))

    fo_y.wait_recv()
    bo_unit(1).wait_recv()
    bo_unit(0).wait_recv()
    for copy in sent:
        copy.wait_send()


def body(segment_input, output_grad, qkv_weight, out_weight, query_gain, key_gain, gate_scale,
         neighbours, tile_slot):
    dma = pltpu.SemaphoreType.DMA
    vm = pltpu.VMEM
    scratch = [
        vm((NZ, 2, 32, D), BF16),
        vm((2, TILE, D), BF16),
        vm((2 * TILE, D), BF16),
        vm((2, D, 3 * HD), BF16),
        vm((NZ, 4, 2, 16, D), BF16),
        vm((2, NZ, TILE, 3 * HD), F32),
        vm((NZ, TILE, 3 * HD), F32),
        vm((NZ, 16, HD), F32),
        vm((NZ, HD, HD), BF16),
        vm((NZ, HD, HD), BF16),
        vm((NZ, HD, HD), BF16),
        vm((HD, NZ * HD), BF16),
        vm((HD, NZ * HD), BF16),
        vm((NZ, NZ * HD, HD), BF16),
        vm((NZ, HD, HD), BF16),
        vm((HD, NZ * HD), BF16),
        vm((NZ, HD, HD), BF16),
        vm((NZ, HD, HD), BF16),
        vm((NZ, HD, HD), F32),
        vm((NZ * HD, HD), F32),
        vm((NZ * HD, HD), F32),
        vm((NZ, TILE, 3 * HD), BF16),
        vm((NZ, TILE, 3 * HD), BF16),
        vm((NZ, TILE, 3 * HD), BF16),
        vm((2, TILE, D), F32),
        vm((2, 7, 32, D), BF16),
        vm((2, 7, 32, D), BF16),
        vm((2, TILE, D), F32),
        vm((TILE, D), F32),
        vm((TILE, D), BF16),
        vm((2, 32, D), BF16),
        vm((16, 8, 192), F32),
        vm((16, 8, 192), F32),
        dma((4,)), dma((2, 7)), dma((2, 7)), dma((2, 4)), dma((2, 4)), dma((NZ, 4)), dma((NZ, 4)),
        dma((NZ,)), dma((NZ,)), dma((4,)), dma((4,)), dma((NZ,)), dma((NZ,)), dma((NZ,)), dma((NZ,)),
        dma((2, 7)), dma((2, 7)), dma((3,)), dma((3,)), dma((16,)), dma((16,)),
    ]
    any_spec = pl.BlockSpec(memory_space=pl.ANY)
    vm_spec = pl.BlockSpec(memory_space=pltpu.VMEM)
    fwd, bwd, gate = pl.pallas_call(
        kernel,
        name="section",
        out_shape=(
            jax.ShapeDtypeStruct((TILE, D), BF16),
            jax.ShapeDtypeStruct((2, 32, D), BF16),
            jax.ShapeDtypeStruct((1, 192), F32),
        ),
        in_specs=[any_spec] * 4 + [vm_spec] * 5,
        out_specs=(any_spec, any_spec, vm_spec),
        scratch_shapes=scratch,
        compiler_params=pltpu.CompilerParams(
            collective_id=0, has_side_effects=True, vmem_limit_bytes=56 * 1024 * 1024),
    )(
        segment_input.reshape(2, 32, D),
        output_grad.reshape(TILE, D),
        qkv_weight.reshape(D, 3 * HD),
        out_weight.reshape(4, 2, 16, D),
        query_gain, key_gain, gate_scale, neighbours, tile_slot[None],
    )
    return fwd[None], bwd.reshape(1, TILE, D), gate


def solution(mesh):
    in_specs = (
        P("pipe", ("dp", "seq"), None),
        P("pipe", ("dp", "seq"), None),
        P("pipe", None, "seq", None),
        P("pipe", "seq", None),
        P("pipe", None),
        P("pipe", None),
        P("pipe", None),
        P("dp", None),
        P("dp"),
    )
    out_specs = (
        P("pipe", ("dp", "seq"), None),
        P("pipe", ("dp", "seq"), None),
        P(("dp", "pipe"), "seq"),
    )
    return jax.shard_map(body, mesh=mesh, in_specs=in_specs, out_specs=out_specs, check_vma=False)
```

time: 514 us -> 141 us (0.27)
  waiting for transfers between devices: 224 us -> 0 us
  Pallas kernels: 0 us -> 135 us
  other arithmetic: 108 us -> 0 us
  matrix products: 85.4 us -> 0 us
  blocking collectives: 46.4 us -> 0 us
  local copies, waits for them, and re-layouts: 26.4 us -> 4.76 us
  between operations: 14.8 us -> 0.64 us
    reduce_scatter x2 -> x0, waiting for transfers between devices: 139 us -> none  [the longest x1 80.7 us: body(): lax.psum_scatter(jnp.dot(rows, out_local, preferred_element_type=jnp.floa...]
    pallas_call x0 -> x1, Pallas kernels: none -> 135 us  [body(): pl.pallas_call(kernel, name='section', out_shape=(jax.ShapeDtypeStruct((T...]
    scatter-add x4 -> x0, other arithmetic: 93 us -> none  [the longest x2 46.5 us: per_block(): value_total.at[block_slots].add(value_part.reshape(block_shape))]
    all_gather x2 -> x0, waiting for transfers between devices: 84.2 us -> none  [the longest x1 45.7 us: body(): lax.all_gather(stream, 'seq', axis=0, tiled=True)]
    dot_general x14 -> x0, matrix products: 74.7 us -> none  [the longest x2 17.5 us: per_block(): jnp.einsum('ahij,aihd->ajhd', score_grad, query_block, preferred_element_...]
    unnamed x1 -> x0, blocking collectives: 46.4 us -> none
    gather x4 -> x0, local copies, waits for them, and re-layouts: 11.6 us -> none  [gathered(): picked = tiles_array[block_slots]]
    sub x2 -> x0, matrix products: 10.6 us -> none  [probabilities(): weights = jnp.exp(scores - row_max)]
  transfers between devices with their start and end apart: 6 -> 0, of which waited for: 4 -> 0; matrix products, arithmetic and copies ran while one was open for 4% -> 0% of each run, Pallas kernels for 0% -> 0%
where the time goes in v1:
time: 141 us; the launch traced here: 140 us
  Pallas kernels  135 us (96%)
  local copies, waits for them, and re-layouts  4.76 us (3%)
    pallas_call x1, Pallas kernels, body(): pl.pallas_call(kernel, name='section', out_shape=(jax.ShapeDtypeStruct((T...  135 us
    unnamed x3, local copies, waits for them, and re-layouts  4.76 us

profile of v1, /device:TPU:8, one launch (start us, length us, event | category | flops | bytes accessed | tf_op | source)
XLA Modules:
  0.0 140.3 jit_solution(12523888596812426143)
XLA Ops:
  0.6 134.9 %section.1 = (bf16[64,3072]{1,0:T(8,128)(2,1)}, bf16[2,32,3072]{2,1,0:T(8,128)(2,1)}, f32[1,192]{1,0:T(1,128)}) custom-call(bf16[2,32,3072]{2,1,0:T(8,128)(2,1)} %bitcast.11, bf16[64,3072]{1,0:T(8,128)(2,1)} %bitcast.12, bf16[3072,384]{1,0:T(8,128)(2,1)} %bitcast.7, bf16[4,2,16,3072]{3,2,1,0:T(8,128)(2,1)} %bitcast.8, f32[1,128]{1,0:T(1,128)} %qgain.1, ...), custom_call_target="tpu_custom_call" | custom-call | tf_op jit(solution)/shard_map/section/pallas_call | solution.py:471
  135.6 1.8 %copy.15 = bf16[1,64,3072]{2,1,0:T(8,128)(2,1)} copy(bf16[1,64,3072]{2,1,0:T(8,128)(2,1)} %bitcast.10) | data formatting | bytes 786432
  137.4 1.8 %copy.16 = bf16[1,64,3072]{2,1,0:T(8,128)(2,1)} copy(bf16[1,64,3072]{2,1,0:T(8,128)(2,1)} %bitcast.9) | data formatting | bytes 786432
  139.1 1.2 copy.17

commit v2 on v1

v2 whole, which is shorter than its diff:
```python
import functools
import math

import jax
import jax.numpy as jnp
from jax import lax
from jax.experimental import pallas as pl
from jax.experimental.pallas import tpu as pltpu
from jax.sharding import PartitionSpec as P

EPSILON = 1e-06
MESH = pl.DeviceIdType.MESH
F32 = jnp.float32
BF16 = jnp.bfloat16
D = 3072
HD = 128
TILE = 64
NZ = 8
QB = 256
NQ = 4
COLS = 512
NT = (((1,), (1,)), ((), ()))


def dot(a, b):
    return jnp.dot(a, b, preferred_element_type=F32)


def dot_nt(a, b):
    return lax.dot_general(a, b, NT, preferred_element_type=F32)


def kernel(
    stream, upstream, wqkv, wout, qgain, kgain, gate, neigh, tslot,
    fwd_out, bwd_out, gate_out,
    Sg, UP, SC, WQ, WO, PJX, PJ1, BIAS, Qb, Kb, Vb, KT, VT, Pb, ATT, AH, DOS, DO,
    dQ, dK, dV, PG, PGX, WT, GT, SB, RB, AOUT, AOX, FO, BO, GS, GR,
    ld, zs_s, zs_r, zw_s, zw_r, xw_s, xw_r, pj_s, pj_r, ex_s, ex_r,
    at_s, at_r, do_s, do_r, pg_s, pg_r, rs_s, rs_r, y_s, y_r, g_s, g_r,
):
    seq = lax.axis_index("seq")
    x = lax.axis_index("dp")
    y = lax.axis_index("pipe")
    z = lax.div(seq, 2)
    c = lax.rem(seq, 2)

    def dev(d, e=0):
        return {"seq": 2 * lax.rem(z + d, NZ) + (c if e == 0 else 1 - c)}

    right, left, partner = dev(1), dev(NZ - 1), dev(0, 1)
    xr = {"dp": lax.rem(x + 1, 4)}
    xl = {"dp": lax.rem(x + 3, 4)}
    yn = {"pipe": lax.rem(y + 1, 4)}
    yp = {"pipe": lax.rem(y + 3, 4)}

    sent = []

    def remote(src, dst, ssem, rsem, to):
        return pltpu.make_async_remote_copy(
            src_ref=src, dst_ref=dst, send_sem=ssem, recv_sem=rsem,
            device_id=to, device_id_type=MESH)

    def go(copy):
        copy.start()
        sent.append(copy)

    loads = [
        pltpu.make_async_copy(wout, WO.at[0], ld.at[0]),
        pltpu.make_async_copy(stream, Sg.at[0], ld.at[1]),
        pltpu.make_async_copy(upstream, UP.at[0], ld.at[2]),
        pltpu.make_async_copy(wqkv, WQ.at[0], ld.at[3]),
    ]
    for copy in loads:
        copy.start()

    barrier = pltpu.get_barrier_semaphore()
    peers = [right, left, partner, xr, xl, yn, yp]
    for peer in peers:
        pl.semaphore_signal(barrier, inc=1, device_id=peer, device_id_type=MESH)
    pl.semaphore_wait(barrier, len(peers))

    def at(way, j):
        return (NZ - j) % NZ if way == 0 else j % NZ

    def ring_to(way):
        return right if way == 0 else left

    def s_unit(way, k):
        j, half = k // 2, (k + way) % 2
        return remote(Sg.at[at(way, j), half], Sg.at[at(way, j + 1), half],
                      zs_s.at[way, k], zs_r.at[way, k], ring_to(way))

    def w_unit(way, k):
        j, half = k // 2, (k + way) % 2
        return remote(WO.at[at(way, j), x, half], WO.at[at(way, j + 1), x, half],
                      zw_s.at[way, k], zw_r.at[way, k], ring_to(way))

    def x_unit(d, way, part):
        quarter = x if part < 2 else lax.rem(x + (3 if way == 0 else 1), 4)
        ref = WO.at[d, quarter, part if part < 2 else way]
        return remote(ref, ref, xw_s.at[d, way, part], xw_r.at[d, way, part], xr if way == 0 else xl)

    def s_wait(k):
        for way in (0, 1):
            s_unit(way, k).wait_recv()

    def s_next(k):
        s_wait(k)
        if k + 2 <= 6:
            for way in (0, 1):
                go(s_unit(way, k + 2))

    def w_next(k):
        for way in (0, 1):
            w_unit(way, k).wait_recv()
            if k + 2 <= 6:
                go(w_unit(way, k + 2))

    def x_send(d, half):
        for way in (0, 1):
            go(x_unit(d, way, half))

    def x_next(d, way):
        x_unit(d, way, way).wait_recv()
        go(x_unit(d, way, 2))

    def x_done(d):
        for way in (0, 1):
            x_unit(d, way, 1 - way).wait_recv()
            x_unit(d, way, 2).wait_recv()

    def project(ds):
        rows = [Sg.at[d] for d in ds]

        def one(e, carry):
            lhs = [r[...].reshape(TILE, D) for r in rows]
            lhs = lhs[0] if len(lhs) == 1 else jnp.concatenate(lhs, axis=0)
            out = dot(lhs, WQ[e])
            for n, d in enumerate(ds):
                PJX[e, d] = out[n * TILE:(n + 1) * TILE]
            return carry

        lax.fori_loop(0, 2, one, 0)
        for d in ds:
            go(pj_unit(d))

    def pj_unit(d):
        return remote(PJX.at[1, d], PJ1.at[d], pj_s.at[d], pj_r.at[d], partner)

    def do_unit(d):
        return remote(DOS.at[d], DO.at[(NZ - d) % NZ], do_s.at[d], do_r.at[d], dev(d))

    def grads_in(ds):
        for d in ds:
            val = dot_nt(SC[...], WO[d].reshape(HD, D)).astype(BF16)
            if d == 0:
                DO[0] = val
            else:
                DOS[d] = val
                go(do_unit(d))

    up_x = remote(UP.at[0], UP.at[1], ex_s.at[0], ex_r.at[0], partner)
    wq_x = remote(WQ.at[0], WQ.at[1], ex_s.at[1], ex_r.at[1], partner)

    loads[0].wait()
    for k in (0, 1):
        for way in (0, 1):
            go(w_unit(way, k))
    loads[1].wait()
    for k in (0, 1):
        for way in (0, 1):
            go(s_unit(way, k))
    loads[2].wait()
    go(up_x)
    loads[3].wait()
    go(wq_x)

    i_rows = lax.broadcasted_iota(jnp.int32, (16, 16), 0)
    rel_z = z + lax.div(i_rows, 2)
    rel_z = jnp.where(rel_z >= NZ, rel_z - NZ, rel_z)
    odd = lax.rem(i_rows, 2)
    rel_slot = 2 * rel_z + jnp.where(odd == 0, c, 1 - c)
    lanes16 = lax.broadcasted_iota(jnp.int32, (16, 16), 1)
    listed = jnp.zeros((16, 16), F32)
    for k in range(neigh.shape[1]):
        listed = listed + jnp.where(neigh[:, k:k + 1] == lanes16, 1.0, 0.0)
    holds = jnp.where(rel_slot == tslot[...], 1.0, 0.0)
    by_key = dot_nt(holds, listed)
    by_key = dot_nt(by_key, holds)
    spread = jnp.where(
        lax.div(lax.broadcasted_iota(jnp.int32, (16, 1024), 1), TILE)
        == lax.broadcasted_iota(jnp.int32, (16, 1024), 0), 1.0, 0.0)
    bias = jnp.where(dot(by_key, spread) > 0.5, 0.0, -jnp.inf)
    for n in range(NQ):
        BIAS[n] = bias[:, n * QB:(n + 1) * QB]

    def both(d):
        return jnp.concatenate([PJX[0, d], PJ1[d]], axis=0)

    def unit_of(part):
        spread = jnp.sqrt(jnp.mean(part * part, axis=-1, keepdims=True) + EPSILON)
        return part / spread, spread

    def norm(ds):
        for d in ds:
            pj_unit(d).wait_recv()
            pj = both(d)
            q_unit, _ = unit_of(pj[:, :HD])
            k_unit, _ = unit_of(pj[:, HD:2 * HD])
            Qb[d] = (q_unit * qgain[...]).astype(BF16)
            k = k_unit * kgain[...]
            v = pj[:, 2 * HD:]
            Kb[d] = k.astype(BF16)
            Vb[d] = v.astype(BF16)
            KT[:, d * HD:(d + 1) * HD] = k.T.astype(BF16)
            VT[:, d * HD:(d + 1) * HD] = v.T.astype(BF16)

    w_next(0)
    x_send(7, 0)
    x_send(1, 1)
    up_x.wait_recv()
    SC[...] = (UP[...].astype(F32) * gate[...]).astype(BF16).reshape(2 * TILE, D)
    w_next(1)
    x_send(7, 1)
    x_send(1, 0)
    wq_x.wait_recv()
    project([0])
    x_next(7, 0)
    x_next(1, 1)
    s_next(0)
    grads_in([0])
    x_next(1, 0)
    x_next(7, 1)

    def flip(e):
        def one(n, carry):
            rows = pl.ds(pl.multiple_of(n * COLS, COLS), COLS)
            WT[e * 3 * HD:(e + 1) * 3 * HD, rows] = WQ[e, rows, :].T
            return carry

        lax.fori_loop(0, D // COLS, one, 0)

    s_next(1)
    project([7, 1])
    w_next(2)
    x_send(6, 0)
    x_send(2, 1)
    x_done(7)
    x_done(1)
    w_next(3)
    x_send(6, 1)
    x_send(2, 0)
    grads_in([7, 1])
    x_next(6, 0)
    x_next(2, 1)
    flip(0)
    s_next(2)
    norm([0, 7, 1])
    x_next(2, 0)
    x_next(6, 1)
    s_next(3)
    project([6, 2])
    w_next(4)
    x_send(5, 0)
    x_send(3, 1)
    x_done(6)
    x_done(2)
    w_next(5)
    x_send(5, 1)
    x_send(3, 0)
    grads_in([6, 2])
    x_next(5, 0)
    x_next(3, 1)
    flip(1)
    s_next(4)
    norm([6, 2])
    x_next(3, 0)
    x_next(5, 1)
    s_next(5)
    project([5, 3])
    w_next(6)
    x_send(4, 0)
    x_send(4, 1)
    x_done(5)
    x_done(3)
    grads_in([5, 3])
    x_next(4, 0)
    x_next(4, 1)
    norm([5, 3])
    s_next(6)
    project([4])
    norm([4])
    scale = 1.0 / math.sqrt(HD)

    def block(ref, n):
        return ref[pl.ds(2 * n, 2)].reshape(QB, HD)

    def attend(n, carry):
        s = dot_nt(Kb[...].reshape(NZ * HD, HD), block(Qb, n)) * (scale * math.log2(math.e))
        s = s.reshape(16, TILE, QB) + BIAS[n][:, None, :]
        s = s.reshape(NZ * HD, QB)
        p = jnp.exp2(s - jnp.max(s, axis=0, keepdims=True))
        p = (p * (1.0 / jnp.sum(p, axis=0, keepdims=True))).astype(BF16)
        Pb[n] = p
        ATT[pl.ds(2 * n, 2)] = dot(VT[...], p).T.astype(BF16).reshape(2, HD, HD)
        return carry

    lax.fori_loop(0, 2, attend, 0)
    x_done(4)
    grads_in([4])
    lax.fori_loop(2, NQ, attend, 0)

    def at_unit(d):
        back = (NZ - d) % NZ
        return remote(ATT.at[d], AH.at[:, back * HD:(back + 1) * HD], at_s.at[d], at_r.at[d], dev(d))

    for d in range(1, NZ):
        go(at_unit(d))
    AH[:, :HD] = ATT[0]
    dK[...] = jnp.zeros_like(dK)
    dV[...] = jnp.zeros_like(dV)
    for d in range(1, NZ):
        do_unit(d).wait_recv()

    def attend_back(n, carry):
        grad, p = block(DO, n), Pb[n]
        dV[...] += dot(p, grad)
        dp = dot_nt(Vb[...].reshape(NZ * HD, HD), grad)
        wide = p.astype(F32)
        delta = jnp.sum(wide * dp, axis=0, keepdims=True)
        ds = (wide * (dp - delta) * scale).astype(BF16)
        dK[...] += dot(ds, block(Qb, n))
        dQ[pl.ds(2 * n, 2)] = dot(KT[...], ds).T.reshape(2, HD, HD)
        return carry

    lax.fori_loop(0, NQ, attend_back, 0)

    def norm_back(ds):
        for d in ds:
            pj = both(d)

            def one(part, grad, gain):
                unit, spread = unit_of(part)
                a = grad * gain
                return (a - unit * jnp.mean(a * unit, axis=-1, keepdims=True)) / spread

            gq = one(pj[:, :HD], dQ[d], qgain[...])
            gk = one(pj[:, HD:2 * HD], dK[d * HD:(d + 1) * HD, :], kgain[...])
            pg = jnp.concatenate([gq, gk, dV[d * HD:(d + 1) * HD, :]], axis=1).astype(BF16)
            PG[d, :, :3 * HD] = pg[:TILE]
            PGX[d] = pg[TILE:]
            go(pg_unit(d))

    def pg_unit(d):
        return remote(PGX.at[d], PG.at[d, :, 3 * HD:], pg_s.at[d], pg_r.at[d], partner)

    norm_back([4, 3, 5])

    def group(ds):
        for d in ds:
            pg_unit(d).wait_recv()

        def one(n, carry):
            cols = pl.ds(pl.multiple_of(n * COLS, COLS), COLS)
            rows = jnp.concatenate([PG[d] for d in ds], axis=0)
            out = dot(rows, WT[:, cols])
            for i, d in enumerate(ds):
                GT[d, :, cols] = out[i * TILE:(i + 1) * TILE]
            return carry

        lax.fori_loop(0, D // COLS, one, 0)

    ends = [(1, 2), (1, 3), (1, 0), (1, 1)]
    plan = [
        [(4, 0), (4, 1), (3, 2), (3, 3), (3, 0), (3, 1), (2, 2), (2, 3), (2, 0), (2, 1)] + ends,
        [(4, 2), (4, 3), (3, 0), (3, 1), (3, 2), (3, 3), (2, 0), (2, 1), (2, 2), (2, 3)] + ends,
    ]

    def rs_unit(way, k):
        return remote(SB.at[way, k], RB.at[way, k], rs_s.at[way, k], rs_r.at[way, k], ring_to(way))

    def rs_send(k):
        for way in (0, 1):
            dist, q = plan[way][k]
            val = GT[dist if way == 0 else NZ - dist, q * 16:(q + 1) * 16, :]
            if (dist + 1, q) in plan[way]:
                needs = plan[way].index((dist + 1, q))
                rs_unit(way, needs).wait_recv()
                val = val + RB[way, needs].astype(F32)
            SB[way, k] = val.astype(BF16)
            go(rs_unit(way, k))

    group([4, 3, 5])
    rs_send(0)
    rs_send(1)
    rs_send(2)
    rs_send(3)
    norm_back([2, 6, 1, 7, 0])
    rs_send(4)
    rs_send(5)
    group([2, 6, 1, 7, 0])
    rs_send(6)
    rs_send(7)

    for d in range(1, NZ):
        at_unit(d).wait_recv()

    def out_proj(n, carry):
        cols = pl.ds(pl.multiple_of(n * COLS, COLS), COLS)
        w = WO[:, :, :, :, cols].reshape(NZ * HD, COLS)
        out = dot(AH[...], w)
        AOUT[0, :, cols] = out[:TILE]
        AOUT[1, :, cols] = out[TILE:]
        return carry

    lax.fori_loop(0, 3, out_proj, 0)
    rs_send(8)
    lax.fori_loop(3, D // COLS, out_proj, 0)
    rs_send(9)
    ao_x = remote(AOUT.at[1], AOX, ex_s.at[3], ex_r.at[3], partner)
    go(ao_x)
    ao_x.wait_recv()
    wide_ao = AOUT[0] + AOX[...]
    FO[...] = (Sg[0].reshape(TILE, D).astype(F32) + gate[...] * wide_ao).astype(BF16)
    fo_y = remote(FO, fwd_out, y_s.at[0], y_r.at[0], yn)
    go(fo_y)
    gsum = jnp.sum((UP[0].astype(F32) * wide_ao).reshape(8, 8, D), axis=0)
    for n in range(16):
        GS[n] = gsum[:, n * 192:(n + 1) * 192]

    def g_unit(d, e):
        i = 2 * d + e
        own = dev(d, e)["seq"]
        return remote(GS.at[own], GR.at[2 * ((NZ - d) % NZ) + e], g_s.at[i], g_r.at[i], dev(d, e))

    pairs = [(d, e) for d in range(NZ) for e in range(2) if d or e]
    for d, e in pairs:
        go(g_unit(d, e))
    GR[0] = GS[seq]
    rs_send(10)
    rs_send(11)
    rs_send(12)
    rs_send(13)

    def bo_unit(q):
        return remote(BO.at[q], bwd_out.at[q], y_s.at[1 + q], y_r.at[1 + q], yp)

    for dist, q in ends:
        total = GT[0, q * 16:(q + 1) * 16, :]
        for way in (0, 1):
            k = plan[way].index((dist, q))
            rs_unit(way, k).wait_recv()
            total = total + RB[way, k].astype(F32)
        BO[q] = (UP[0, q * 16:(q + 1) * 16, :].astype(F32) + total).astype(BF16)
        go(bo_unit(q))

    for d, e in pairs:
        g_unit(d, e).wait_recv()
    gate_out[...] = jnp.sum(jnp.sum(GR[...], axis=0), axis=0, keepdims=True)
    fo_y.wait_recv()
    for q in range(4):
        bo_unit(q).wait_recv()
    for copy in sent:
        copy.wait_send()


def body(segment_input, output_grad, qkv_weight, out_weight, query_gain, key_gain, gate_scale,
         neighbours, tile_slot):
    dma = pltpu.SemaphoreType.DMA
    vm = pltpu.VMEM
    scratch = [
        vm((NZ, 2, 32, D), BF16),
        vm((2, TILE, D), BF16),
        vm((2 * TILE, D), BF16),
        vm((2, D, 3 * HD), BF16),
        vm((NZ, 4, 2, 16, D), BF16),
        vm((2, NZ, TILE, 3 * HD), F32),
        vm((NZ, TILE, 3 * HD), F32),
        vm((NQ, 16, QB), F32),
        vm((NZ, HD, HD), BF16),
        vm((NZ, HD, HD), BF16),
        vm((NZ, HD, HD), BF16),
        vm((HD, NZ * HD), BF16),
        vm((HD, NZ * HD), BF16),
        vm((NQ, NZ * HD, QB), BF16),
        vm((NZ, HD, HD), BF16),
        vm((HD, NZ * HD), BF16),
        vm((NZ, HD, HD), BF16),
        vm((NZ, HD, HD), BF16),
        vm((NZ, HD, HD), F32),
        vm((NZ * HD, HD), F32),
        vm((NZ * HD, HD), F32),
        vm((NZ, TILE, 6 * HD), BF16),
        vm((NZ, TILE, 3 * HD), BF16),
        vm((6 * HD, D), BF16),
        vm((NZ, TILE, D), F32),
        vm((2, 14, 16, D), BF16),
        vm((2, 14, 16, D), BF16),
        vm((2, TILE, D), F32),
        vm((TILE, D), F32),
        vm((TILE, D), BF16),
        vm((4, 16, D), BF16),
        vm((16, 8, 192), F32),
        vm((16, 8, 192), F32),
        dma((4,)), dma((2, 7)), dma((2, 7)), dma((2, 7)), dma((2, 7)), dma((NZ, 2, 3)), dma((NZ, 2, 3)),
        dma((NZ,)), dma((NZ,)), dma((4,)), dma((4,)), dma((NZ,)), dma((NZ,)), dma((NZ,)), dma((NZ,)),
        dma((NZ,)), dma((NZ,)), dma((2, 14)), dma((2, 14)), dma((5,)), dma((5,)), dma((16,)), dma((16,)),
    ]
    any_spec = pl.BlockSpec(memory_space=pl.ANY)
    vm_spec = pl.BlockSpec(memory_space=pltpu.VMEM)
    fwd, bwd, gate = pl.pallas_call(
        kernel,
        name="section",
        out_shape=(
            jax.ShapeDtypeStruct((TILE, D), BF16),
            jax.ShapeDtypeStruct((4, 16, D), BF16),
            jax.ShapeDtypeStruct((1, 192), F32),
        ),
        in_specs=[any_spec] * 4 + [vm_spec] * 5,
        out_specs=(any_spec, any_spec, vm_spec),
        scratch_shapes=scratch,
        compiler_params=pltpu.CompilerParams(
            collective_id=0, has_side_effects=True, vmem_limit_bytes=56 * 1024 * 1024),
    )(
        segment_input.reshape(2, 32, D),
        output_grad.reshape(TILE, D),
        qkv_weight.reshape(D, 3 * HD),
        out_weight.reshape(4, 2, 16, D),
        query_gain, key_gain, gate_scale, neighbours, tile_slot[None],
    )
    return fwd[None], bwd.reshape(1, TILE, D), gate


def solution(mesh):
    in_specs = (
        P("pipe", ("dp", "seq"), None),
        P("pipe", ("dp", "seq"), None),
        P("pipe", None, "seq", None),
        P("pipe", "seq", None),
        P("pipe", None),
        P("pipe", None),
        P("pipe", None),
        P("dp", None),
        P("dp"),
    )
    out_specs = (
        P("pipe", ("dp", "seq"), None),
        P("pipe", ("dp", "seq"), None),
        P(("dp", "pipe"), "seq"),
    )
    return jax.shard_map(body, mesh=mesh, in_specs=in_specs, out_specs=out_specs, check_vma=False)
```

time: 141 us -> 124 us (0.88)
  Pallas kernels: 135 us -> 117 us
    pallas_call x1, Pallas kernels: 135 us -> 117 us  [body(): pl.pallas_call(kernel, name='section', out_shape=(jax.ShapeDtypeStruct((T...]
where the time goes in v2:
time: 124 us; the launch traced here: 123 us
  Pallas kernels  117 us (94%)
  local copies, waits for them, and re-layouts  4.76 us (4%)
    pallas_call x1, Pallas kernels, body(): pl.pallas_call(kernel, name='section', out_shape=(jax.ShapeDtypeStruct((T...  117 us
    unnamed x3, local copies, waits for them, and re-layouts  4.76 us

profile of v2, /device:TPU:8, one launch (start us, length us, event | category | flops | bytes accessed | tf_op | source)
XLA Modules:
  0.0 122.8 jit_solution(16612741088805893025)
XLA Ops:
  0.6 117.4 %section.1 = (bf16[64,3072]{1,0:T(8,128)(2,1)}, bf16[4,16,3072]{2,1,0:T(8,128)(2,1)}, f32[1,192]{1,0:T(1,128)}) custom-call(bf16[2,32,3072]{2,1,0:T(8,128)(2,1)} %bitcast.11, bf16[64,3072]{1,0:T(8,128)(2,1)} %bitcast.12, bf16[3072,384]{1,0:T(8,128)(2,1)} %bitcast.7, bf16[4,2,16,3072]{3,2,1,0:T(8,128)(2,1)} %bitcast.8, f32[1,128]{1,0:T(1,128)} %qgain.1, ...), custom_call_target="tpu_custom_call" | custom-call | tf_op jit(solution)/shard_map/section/pallas_call | solution.py:511
  118.1 1.8 %copy.15 = bf16[1,64,3072]{2,1,0:T(8,128)(2,1)} copy(bf16[1,64,3072]{2,1,0:T(8,128)(2,1)} %bitcast.10) | data formatting | bytes 786432
  119.8 1.8 %copy.16 = bf16[1,64,3072]{2,1,0:T(8,128)(2,1)} copy(bf16[1,64,3072]{2,1,0:T(8,128)(2,1)} %bitcast.9) | data formatting | bytes 786432
  121.6 1.2 copy.17

commit v3 on v2

--- a/solution.py
+++ b/solution.py
@@ -120,6 +120,11 @@
         for way in (0, 1):
             go(x_unit(d, way, half))
 
+    def x_both(d):
+        for half in (0, 1):
+            for way in (0, 1):
+                go(x_unit(d, way, (half + way) % 2))
+
     def x_next(d, way):
         x_unit(d, way, way).wait_recv()
         go(x_unit(d, way, 2))
@@ -167,9 +172,6 @@
         for way in (0, 1):
             go(w_unit(way, k))
     loads[1].wait()
-    for k in (0, 1):
-        for way in (0, 1):
-            go(s_unit(way, k))
     loads[2].wait()
     go(up_x)
     loads[3].wait()
@@ -215,23 +217,6 @@
             KT[:, d * HD:(d + 1) * HD] = k.T.astype(BF16)
             VT[:, d * HD:(d + 1) * HD] = v.T.astype(BF16)
 
-    w_next(0)
-    x_send(7, 0)
-    x_send(1, 1)
-    up_x.wait_recv()
-    SC[...] = (UP[...].astype(F32) * gate[...]).astype(BF16).reshape(2 * TILE, D)
-    w_next(1)
-    x_send(7, 1)
-    x_send(1, 0)
-    wq_x.wait_recv()
-    project([0])
-    x_next(7, 0)
-    x_next(1, 1)
-    s_next(0)
-    grads_in([0])
-    x_next(1, 0)
-    x_next(7, 1)
-
     def flip(e):
         def one(n, carry):
             rows = pl.ds(pl.multiple_of(n * COLS, COLS), COLS)
@@ -240,52 +225,70 @@
 
         lax.fori_loop(0, D // COLS, one, 0)
 
-    s_next(1)
-    project([7, 1])
+    w_next(0)
+    x_send(7, 0)
+    w_next(1)
+    x_send(7, 1)
+    for k in (0, 1):
+        for way in (0, 1):
+            go(s_unit(way, k))
+    up_x.wait_recv()
+    SC[...] = (UP[...].astype(F32) * gate[...]).astype(BF16).reshape(2 * TILE, D)
+    x_next(7, 0)
     w_next(2)
     x_send(6, 0)
     x_send(2, 1)
-    x_done(7)
-    x_done(1)
+    x_next(7, 1)
     w_next(3)
     x_send(6, 1)
     x_send(2, 0)
-    grads_in([7, 1])
+    wq_x.wait_recv()
+    project([0])
+    grads_in([0])
     x_next(6, 0)
     x_next(2, 1)
-    flip(0)
-    s_next(2)
-    norm([0, 7, 1])
+    s_next(0)
+    x_done(7)
+    grads_in([7])
     x_next(2, 0)
     x_next(6, 1)
-    s_next(3)
-    project([6, 2])
+    s_next(1)
+    project([7, 1])
     w_next(4)
     x_send(5, 0)
     x_send(3, 1)
-    x_done(6)
-    x_done(2)
     w_next(5)
     x_send(5, 1)
     x_send(3, 0)
+    flip(0)
+    x_done(6)
+    x_done(2)
     grads_in([6, 2])
+    s_next(2)
     x_next(5, 0)
     x_next(3, 1)
-    flip(1)
-    s_next(4)
-    norm([6, 2])
+    norm([0, 7, 1])
     x_next(3, 0)
     x_next(5, 1)
-    s_next(5)
-    project([5, 3])
+    s_next(3)
+    project([6, 2])
     w_next(6)
-    x_send(4, 0)
-    x_send(4, 1)
+    x_both(4)
+    x_both(1)
+    flip(1)
     x_done(5)
     x_done(3)
     grads_in([5, 3])
+    s_next(4)
+    norm([6, 2])
     x_next(4, 0)
     x_next(4, 1)
+    s_next(5)
+    project([5, 3])
+    x_next(1, 0)
+    x_next(1, 1)
+    x_done(4)
+    grads_in([4])
     norm([5, 3])
     s_next(6)
     project([4])
@@ -306,8 +309,8 @@
         return carry
 
     lax.fori_loop(0, 2, attend, 0)
-    x_done(4)
-    grads_in([4])
+    x_done(1)
+    grads_in([1])
     lax.fori_loop(2, NQ, attend, 0)
 
     def at_unit(d):
@@ -319,7 +322,7 @@
     AH[:, :HD] = ATT[0]
     dK[...] = jnp.zeros_like(dK)
     dV[...] = jnp.zeros_like(dV)
-    for d in range(1, NZ):
+    for d in (7, 6, 5, 4, 3):
         do_unit(d).wait_recv()
 
     def attend_back(n, carry):
@@ -333,7 +336,10 @@
         dQ[pl.ds(2 * n, 2)] = dot(KT[...], ds).T.reshape(2, HD, HD)
         return carry
 
-    lax.fori_loop(0, NQ, attend_back, 0)
+    lax.fori_loop(0, NQ - 1, attend_back, 0)
+    for d in (2, 1):
+        do_unit(d).wait_recv()
+    attend_back(NQ - 1, 0)
 
     def norm_back(ds):
         for d in ds:
@@ -402,6 +408,9 @@
     rs_send(6)
     rs_send(7)
 
+    rs_send(8)
+    rs_send(9)
+
     for d in range(1, NZ):
         at_unit(d).wait_recv()
 
@@ -413,12 +422,13 @@
         AOUT[1, :, cols] = out[TILE:]
         return carry
 
-    lax.fori_loop(0, 3, out_proj, 0)
-    rs_send(8)
-    lax.fori_loop(3, D // COLS, out_proj, 0)
-    rs_send(9)
+    lax.fori_loop(0, D // COLS, out_proj, 0)
     ao_x = remote(AOUT.at[1], AOX, ex_s.at[3], ex_r.at[3], partner)
     go(ao_x)
+    rs_send(10)
+    rs_send(11)
+    rs_send(12)
+    rs_send(13)
     ao_x.wait_recv()
     wide_ao = AOUT[0] + AOX[...]
     FO[...] = (Sg[0].reshape(TILE, D).astype(F32) + gate[...] * wide_ao).astype(BF16)
@@ -437,10 +447,6 @@
     for d, e in pairs:
         go(g_unit(d, e))
     GR[0] = GS[seq]
-    rs_send(10)
-    rs_send(11)
-    rs_send(12)
-    rs_send(13)
 
     def bo_unit(q):
         return remote(BO.at[q], bwd_out.at[q], y_s.at[1 + q], y_r.at[1 + q], yp)

time: 124 us -> 121 us (0.976)
  Pallas kernels: 117 us -> 115 us
    pallas_call x1, Pallas kernels: 117 us -> 115 us  [body(): pl.pallas_call(kernel, name='section', out_shape=(jax.ShapeDtypeStruct((T...]
where the time goes in v3:
time: 121 us
  Pallas kernels  115 us (95%)
  local copies, waits for them, and re-layouts  4.76 us (4%)
    pallas_call x1, Pallas kernels, body(): pl.pallas_call(kernel, name='section', out_shape=(jax.ShapeDtypeStruct((T...  115 us
    unnamed x3, local copies, waits for them, and re-layouts  4.76 us

profile of v3, /device:TPU:8, one launch (start us, length us, event | category | flops | bytes accessed | tf_op | source)
XLA Modules:
  0.0 120.8 jit_solution(6616233403636055380)
XLA Ops:
  0.6 115.4 %section.1 = (bf16[64,3072]{1,0:T(8,128)(2,1)}, bf16[4,16,3072]{2,1,0:T(8,128)(2,1)}, f32[1,192]{1,0:T(1,128)}) custom-call(bf16[2,32,3072]{2,1,0:T(8,128)(2,1)} %bitcast.11, bf16[64,3072]{1,0:T(8,128)(2,1)} %bitcast.12, bf16[3072,384]{1,0:T(8,128)(2,1)} %bitcast.7, bf16[4,2,16,3072]{3,2,1,0:T(8,128)(2,1)} %bitcast.8, f32[1,128]{1,0:T(1,128)} %qgain.1, ...), custom_call_target="tpu_custom_call" | custom-call | tf_op jit(solution)/shard_map/section/pallas_call | solution.py:517
  116.0 1.8 %copy.15 = bf16[1,64,3072]{2,1,0:T(8,128)(2,1)} copy(bf16[1,64,3072]{2,1,0:T(8,128)(2,1)} %bitcast.10) | data formatting | bytes 786432
  117.8 1.8 %copy.16 = bf16[1,64,3072]{2,1,0:T(8,128)(2,1)} copy(bf16[1,64,3072]{2,1,0:T(8,128)(2,1)} %bitcast.9) | data formatting | bytes 786432
  119.6 1.2 %copy.17 = f32[1,192]{1,0:T(1,128)} copy(f32[1,192]{1,0:T(1,128)} %get-tuple-element.14) | data formatting | bytes 1536

commit v4 on v3

--- a/solution.py
+++ b/solution.py
@@ -32,7 +32,7 @@
 
 def kernel(
     stream, upstream, wqkv, wout, qgain, kgain, gate, neigh, tslot,
-    fwd_out, bwd_out, gate_out,
+    both_out, gate_out,
     Sg, UP, SC, WQ, WO, PJX, PJ1, BIAS, Qb, Kb, Vb, KT, VT, Pb, ATT, AH, DOS, DO,
     dQ, dK, dV, PG, PGX, WT, GT, SB, RB, AOUT, AOX, FO, BO, GS, GR,
     ld, zs_s, zs_r, zw_s, zw_r, xw_s, xw_r, pj_s, pj_r, ex_s, ex_r,
@@ -401,14 +401,16 @@
     rs_send(1)
     rs_send(2)
     rs_send(3)
-    norm_back([2, 6, 1, 7, 0])
+    norm_back([2, 6])
     rs_send(4)
+    norm_back([1, 7])
     rs_send(5)
-    group([2, 6, 1, 7, 0])
+    group([2, 6])
     rs_send(6)
     rs_send(7)
-
+    norm_back([0])
     rs_send(8)
+    group([1, 7, 0])
     rs_send(9)
 
     for d in range(1, NZ):
@@ -432,7 +434,7 @@
     ao_x.wait_recv()
     wide_ao = AOUT[0] + AOX[...]
     FO[...] = (Sg[0].reshape(TILE, D).astype(F32) + gate[...] * wide_ao).astype(BF16)
-    fo_y = remote(FO, fwd_out, y_s.at[0], y_r.at[0], yn)
+    fo_y = remote(FO, both_out.at[0], y_s.at[0], y_r.at[0], yn)
     go(fo_y)
     gsum = jnp.sum((UP[0].astype(F32) * wide_ao).reshape(8, 8, D), axis=0)
     for n in range(16):
@@ -449,7 +451,7 @@
     GR[0] = GS[seq]
 
     def bo_unit(q):
-        return remote(BO.at[q], bwd_out.at[q], y_s.at[1 + q], y_r.at[1 + q], yp)
+        return remote(BO.at[q], both_out.at[1, q * 16:(q + 1) * 16], y_s.at[1 + q], y_r.at[1 + q], yp)
 
     for dist, q in ends:
         total = GT[0, q * 16:(q + 1) * 16, :]
@@ -514,16 +516,15 @@
     ]
     any_spec = pl.BlockSpec(memory_space=pl.ANY)
     vm_spec = pl.BlockSpec(memory_space=pltpu.VMEM)
-    fwd, bwd, gate = pl.pallas_call(
+    out, gate = pl.pallas_call(
         kernel,
         name="section",
         out_shape=(
-            jax.ShapeDtypeStruct((TILE, D), BF16),
-            jax.ShapeDtypeStruct((4, 16, D), BF16),
+            jax.ShapeDtypeStruct((2, TILE, D), BF16),
             jax.ShapeDtypeStruct((1, 192), F32),
         ),
         in_specs=[any_spec] * 4 + [vm_spec] * 5,
-        out_specs=(any_spec, any_spec, vm_spec),
+        out_specs=(any_spec, vm_spec),
         scratch_shapes=scratch,
         compiler_params=pltpu.CompilerParams(
             collective_id=0, has_side_effects=True, vmem_limit_bytes=56 * 1024 * 1024),
@@ -534,7 +535,7 @@
         out_weight.reshape(4, 2, 16, D),
         query_gain, key_gain, gate_scale, neighbours, tile_slot[None],
     )
-    return fwd[None], bwd.reshape(1, TILE, D), gate
+    return out[:1], out[1:], gate
 
 
 def solution(mesh):

time: 121 us -> 119 us (0.983)
  local copies, waits for them, and re-layouts: 4.76 us -> 3.26 us
    unnamed x3 -> x1, local copies, waits for them, and re-layouts: 4.76 us -> 1.22 us
    slice x0 -> x1, local copies, waits for them, and re-layouts: none -> 2.04 us  [body(): return (out[:1], out[1:], gate)]
where the time goes in v4:
time: 119 us
  Pallas kernels  115 us (97%)
  local copies, waits for them, and re-layouts  3.26 us (3%)
    pallas_call x1, Pallas kernels, body(): pl.pallas_call(kernel, name='section', out_shape=(jax.ShapeDtypeStruct((2...  115 us

profile of v4, /device:TPU:8, one launch (start us, length us, event | category | flops | bytes accessed | tf_op | source)
XLA Modules:
  0.0 119.3 jit_solution(131085101983611405)
XLA Ops:
  0.6 115.4 %section.1 = (bf16[2,64,3072]{2,1,0:T(8,128)(2,1)}, f32[1,192]{1,0:T(1,128)}) custom-call(bf16[2,32,3072]{2,1,0:T(8,128)(2,1)} %bitcast.7, bf16[64,3072]{1,0:T(8,128)(2,1)} %bitcast.8, bf16[3072,384]{1,0:T(8,128)(2,1)} %bitcast.5, bf16[4,2,16,3072]{3,2,1,0:T(8,128)(2,1)} %bitcast.6, f32[1,128]{1,0:T(1,128)} %qgain.1, f32[1,128]{1,0:T(1,128)} %kgain.1, ...), custom_call_target="tpu_custom_call" | custom-call | tf_op jit(solution)/shard_map/section/pallas_call | solution.py:519
  116.0 2.0 %fusion = (bf16[1,64,3072]{2,1,0:T(8,128)(2,1)}, bf16[1,64,3072]{2,1,0:T(8,128)(2,1)}) fusion(bf16[2,64,3072]{2,1,0:T(8,128)(2,1)} %get-tuple-element.5), kind=kLoop, calls=%fused_computation | loop fusion | bytes 1572864 | tf_op jit(solution)/shard_map/slice | solution.py:538
  118.1 1.2 %copy.13 = f32[1,192]{1,0:T(1,128)} copy(f32[1,192]{1,0:T(1,128)} %get-tuple-element.14) | data formatting | bytes 1536
